TPU v7x, 128 devices: a whole 4x4x4 slice. The times are simulated.
128 devices in a mesh: dp: 4 (over x_lo, core), expert: 32 (over y, x_hi, z).
Axes of the slice: x: 4 (x_hi: 2, x_lo: 2; x = x_hi * 2 + x_lo), y: 4, z: 4, core: 2. Of those that a mesh axis runs over, the one named last changes fastest.
Arguments:
- hidden_in: bfloat16 [16384, 2048], P(('dp', 'expert')), may hold values from -6 to 6
- attn_gain: float32 [2048], replicated, may hold values from 0.1 to 1.9
- query_key_value_weight: bfloat16 [2048, 2560], P('expert'), may hold values from -0.125 to 0.125
- q_gain: float32 [128], replicated, may hold values from 0.1 to 1.9
- key_norm_gain: float32 [128], replicated, may hold values from 0.1 to 1.9
- w_out: bfloat16 [2048, 2048], P('expert'), may hold values from -0.125 to 0.125
- moe_gain: float32 [2048], replicated, may hold values from 0.1 to 1.9
- w_gate_up: bfloat16 [128, 2048, 1536], P(('dp', 'expert')), may hold values from -0.125 to 0.125
- w_down: bfloat16 [128, 768, 2048], P(('dp', 'expert')), may hold values from -0.21875 to 0.21875
- kv_pool: bfloat16 [32, 2, 128, 2, 128], P('dp'), may hold values from -160 to 160
- page_table: int32 [32], replicated, may hold values from 0 to 31, each once
- suffix_lengths: int32 [4, 4], replicated, may hold values from 1 to 2560, 4096 in all within a row
- request_group: int32 [4, 4], replicated, may hold values from 0 to 1
- expert_ids: int32 [16384, 8], P(('dp', 'expert')), may hold values from 0 to 127, all different within a row; in each aligned block of 128 rows (0 to 127, 128 to 255, ...) at most 12 rows name the same one
- gate_weights: float32 [16384, 8], P(('dp', 'expert')), may hold values from 0.05 to 0.3
Outputs:
- hidden_out: bfloat16 [16384, 2048], P(('dp', 'expert'))
- suffix_cache: bfloat16 [16384, 512], P(('dp', 'expert'))
Inputs may be any that keep to these rules, and one draw needn't show every extreme that they name: page_table holds each pool page once. `suffix_lengths`: each row sums to 4096; the largest of each row is exactly 2560. `expert_ids`: a token's 8 experts differ; among the 128 rows of one device no expert is named more than 12 times, and that many times in some device.
All inputs are finite; a program needn't handle non-finite values.
Results may differ from a plain program's by a relative error of at most 0.01.
The roundings to bfloat16 on the way count: a program that leaves them out, or rounds other values in their place, can miss the bound.
Values may be sent and summed in bfloat16 or wider, within the bound.
A program may use at most 256 MiB of HBM per device.

v0:
```python
import math
import jax
import jax.numpy as jnp
from jax import lax
from jax.sharding import PartitionSpec as P

PREFIX_TOKENS = 2048
PAGE_TOKENS = 128
eps = 1e-06
theta = 1000000.0
floor_value = -1e30


def root_mean_scale(value_rows, gain):
    value_rows = value_rows.astype(jnp.float32)
    return (
        value_rows
        * lax.rsqrt(jnp.mean(value_rows * value_rows, axis=-1, keepdims=True) + eps)
        * gain
    )


def rotary_apply(value_rows, token_positions):
    half = value_rows.shape[-1] // 2
    freqs = theta ** (-jnp.arange(half, dtype=jnp.float32) / half)
    angles = token_positions.astype(jnp.float32)[:, None] * freqs[None, :]
    cosine = jnp.cos(angles)[:, None, :]
    sine = jnp.sin(angles)[:, None, :]
    first = value_rows[..., :half]
    second_split = value_rows[..., half:]
    return jnp.concatenate(
        [first * cosine - second_split * sine, second_split * cosine + first * sine], axis=-1
    )


def layout(lengths_row, index):
    ends = jnp.cumsum(lengths_row)
    starts = ends - lengths_row
    request = jnp.sum((index[:, None] >= ends[None, :]).astype(jnp.int32), axis=1)
    chosen = request[:, None] == jnp.arange(lengths_row.shape[0], dtype=jnp.int32)[None, :]
    offset = index - jnp.sum(jnp.where(chosen, starts[None, :], 0), axis=1)
    return (request, offset, chosen)


def attend(carry, queries, key_rows, value_rows, mask, scale):
    high, total, acc = carry
    scores = (
        jnp.einsum("qkgd,skd->kgqs", queries, key_rows, preferred_element_type=jnp.float32) * scale
    )
    scores = jnp.where(mask[None, None], scores, -jnp.inf)
    new_high = jnp.maximum(high, jnp.max(scores, axis=-1))
    weights = jnp.exp(scores - new_high[..., None])
    scale_factor = jnp.exp(high - new_high)
    total = total * scale_factor + jnp.sum(weights, axis=-1)
    acc = acc * scale_factor[..., None] + jnp.einsum(
        "kgqs,skd->kgqd",
        weights.astype(jnp.bfloat16),
        value_rows,
        preferred_element_type=jnp.float32,
    )
    return (new_high, total, acc)


def expert_rows(rows, gate_up, down):
    both = jnp.dot(rows, gate_up, preferred_element_type=jnp.float32)
    half = both.shape[1] // 2
    act = (jax.nn.silu(both[:, :half]) * both[:, half:]).astype(jnp.bfloat16)
    return jnp.dot(act, down, preferred_element_type=jnp.float32).astype(jnp.bfloat16)


def local(
    hidden_in,
    attn_gain,
    query_key_value_weight,
    q_gain,
    key_norm_gain,
    w_out,
    moe_gain,
    w_gate_up,
    w_down,
    kv_pool,
    page_table,
    suffix_lengths,
    request_group,
    expert_ids,
    gate_weights,
):
    tokens_here, width = hidden_in.shape
    page_rows = kv_pool.shape[2]
    kv_heads = kv_pool.shape[3]
    head_dim = kv_pool.shape[4]
    key_value_width = kv_heads * head_dim
    query_width = query_key_value_weight.shape[1] - 2 * key_value_width
    q_heads = query_width // head_dim
    head_split = q_heads // kv_heads
    scale = 1.0 / math.sqrt(head_dim)
    row_count = lax.axis_size("dp")
    col_count = lax.axis_size("expert")
    row = lax.axis_index("dp")
    col = lax.axis_index("expert")
    normed = root_mean_scale(hidden_in, attn_gain).astype(jnp.bfloat16)
    part = normed
    qkv = jnp.dot(
        part,
        lax.all_gather(query_key_value_weight, "expert", axis=0, tiled=True),
        preferred_element_type=jnp.float32,
    )
    index = col * tokens_here + jnp.arange(tokens_here, dtype=jnp.int32)
    lengths_row = lax.dynamic_index_in_dim(suffix_lengths, row, 0, keepdims=False)
    groups_row = lax.dynamic_index_in_dim(request_group, row, 0, keepdims=False)
    request, offset, chosen = layout(lengths_row, index)
    qgroup = jnp.sum(jnp.where(chosen, groups_row[None, :], 0), axis=1)
    token_positions = PREFIX_TOKENS + offset
    queries = rotary_apply(
        root_mean_scale(qkv[:, :query_width].reshape(tokens_here, q_heads, head_dim), q_gain),
        token_positions,
    ).astype(jnp.bfloat16)
    key_rows = rotary_apply(
        root_mean_scale(
            qkv[:, query_width : query_width + key_value_width].reshape(
                tokens_here, kv_heads, head_dim
            ),
            key_norm_gain,
        ),
        token_positions,
    ).astype(jnp.bfloat16)
    value_rows = (
        qkv[:, query_width + key_value_width :]
        .reshape(tokens_here, kv_heads, head_dim)
        .astype(jnp.bfloat16)
    )
    suffix_cache = jnp.concatenate(
        [
            key_rows.reshape(tokens_here, key_value_width),
            value_rows.reshape(tokens_here, key_value_width),
        ],
        axis=1,
    )
    grouped = queries.reshape(tokens_here, kv_heads, head_split, head_dim)
    carry = (
        jnp.full((kv_heads, head_split, tokens_here), floor_value, jnp.float32),
        jnp.zeros((kv_heads, head_split, tokens_here), jnp.float32),
        jnp.zeros((kv_heads, head_split, tokens_here, head_dim), jnp.float32),
    )
    piece_keys = lax.all_gather(key_rows, "expert", axis=0, tiled=True)
    piece_values = lax.all_gather(value_rows, "expert", axis=0, tiled=True)
    key_index = jnp.arange(piece_keys.shape[0], dtype=jnp.int32)
    key_request, _, _ = layout(lengths_row, key_index)
    mask = (key_request[None, :] == request[:, None]) & (key_index[None, :] <= index[:, None])
    carry = attend(carry, grouped, piece_keys, piece_values, mask, scale)
    per_group = PREFIX_TOKENS // PAGE_TOKENS
    slot_ids = jnp.arange(page_table.shape[0], dtype=jnp.int32)
    piece = lax.all_gather(kv_pool, "dp", axis=0, tiled=True)
    count = piece.shape[0]
    hit = page_table[None, :] == jnp.arange(count, dtype=jnp.int32)[:, None]
    key_group = jnp.repeat(
        jnp.sum(jnp.where(hit, slot_ids[None, :] // per_group, 0), axis=1), page_rows
    )
    mask = key_group[None, :] == qgroup[:, None]
    carry = attend(
        carry,
        grouped,
        piece[:, 0].reshape(count * page_rows, kv_heads, head_dim),
        piece[:, 1].reshape(count * page_rows, kv_heads, head_dim),
        mask,
        scale,
    )
    mixed = (
        (carry[2] / carry[1][..., None])
        .transpose(2, 0, 1, 3)
        .reshape(tokens_here, query_width)
        .astype(jnp.bfloat16)
    )
    part = mixed
    projected = jnp.dot(
        part,
        lax.all_gather(w_out, "expert", axis=0, tiled=True),
        preferred_element_type=jnp.float32,
    )
    mid = (hidden_in.astype(jnp.float32) + projected).astype(jnp.bfloat16)
    moe_in = root_mean_scale(mid, moe_gain).astype(jnp.bfloat16)
    top_k = expert_ids.shape[1]
    expert_count = row_count * col_count
    capacity = max(2, tokens_here * top_k * 3 // (2 * expert_count))
    flat = expert_ids.reshape(-1)
    onehot = (flat[:, None] == jnp.arange(expert_count, dtype=jnp.int32)[None, :]).astype(jnp.int32)
    slot = jnp.sum((jnp.cumsum(onehot, axis=0) - onehot) * onehot, axis=1)
    place = flat * capacity + slot
    sources = jnp.repeat(moe_in, top_k, axis=0)
    outgoing = jnp.zeros((expert_count * capacity, width), jnp.bfloat16).at[place].set(sources)
    gate_up = w_gate_up[0]
    down = w_down[0]
    received = lax.all_to_all(
        outgoing.reshape(expert_count, capacity, width),
        ("dp", "expert"),
        split_axis=0,
        concat_axis=0,
        tiled=True,
    )
    results = expert_rows(received.reshape(-1, width), gate_up, down).reshape(received.shape)
    returned = lax.all_to_all(results, ("dp", "expert"), split_axis=0, concat_axis=0, tiled=True)
    picked = returned.reshape(expert_count * capacity, width)[place].astype(jnp.float32)
    moe = jnp.sum(picked.reshape(tokens_here, top_k, width) * gate_weights[:, :, None], axis=1)
    hidden_out = (mid.astype(jnp.float32) + moe).astype(jnp.bfloat16)
    return (hidden_out, suffix_cache)


def solution(mesh):
    return jax.shard_map(
        local,
        mesh=mesh,
        in_specs=(
            P(("dp", "expert"), None),
            P(),
            P("expert", None),
            P(),
            P(),
            P("expert", None),
            P(),
            P(("dp", "expert"), None, None),
            P(("dp", "expert"), None, None),
            P("dp", None, None, None, None),
            P(),
            P(),
            P(),
            P(("dp", "expert"), None),
            P(("dp", "expert"), None),
        ),
        out_specs=(P(("dp", "expert"), None), P(("dp", "expert"), None)),
        check_vma=False,
    )
```

profile of v0, /device:TPU:67, one launch (start us, length us, event | category | flops | bytes accessed | tf_op | source)
XLA Modules:
  0.0 756.2 jit_solution(2184994517330569896)
XLA Ops:
  8.0 2.6 copy.97
  12.4 1.2 fusion.65
  14.0 114.5 %all-gather.6.cloned.1.call-done = bf16[2048,2560]{1,0:T(8,128)(2,1)} async-done(((bf16[64,2560]{1,0:T(8,128)(2,1)}), bf16[2048,2560]{1,0:T(8,128)(2,1)}) %all-gather.6.cloned.1.call-update) | async-done | bytes 10485776 | tf_op jit(solution)/shard_map/all_gather | solution.py:105
  128.5 5.7 fusion.68
  134.3 1.1 copy-done.8
  136.0 1.6 reshape.345
  137.7 1.1 multiply_reduce_fusion.2
  140.6 0.9 slice.85
  143.5 0.8 copy-done.11
  144.3 1.9 broadcast_add_fusion
  146.4 1.9 copy.104
  148.5 1.4 fusion.71
  150.1 1.2 broadcast_compare_fusion
  151.2 3.1 fusion.29
  154.3 21.2 %all-gather.12.cloned.1.call-done = bf16[32,2,128,2,128]{4,2,3,1,0:T(8,128)(2,1)} async-done(((bf16[8,2,128,2,128]{4,2,3,1,0:T(8,128)(2,1)}), bf16[32,2,128,2,128]{4,2,3,1,0:T(8,128)(2,1)}) %all-gather.12.cloned.1.call-update) | async-done | bytes 4194320 | tf_op jit(solution)/shard_map/all_gather | solution.py:153
  175.5 4.1 fusion.94
  179.6 1.6 copy.98
  181.2 4.6 copy.99
  185.8 4.2 reshape.374
  190.0 1.3 slice_bitcast_fusion
  191.5 1.0 copy-done.6
  193.1 1.7 multiply_multiply_fusion
  196.5 13.6 %bitcast_reduce_fusion = (f32[2,8,128]{2,1,0:T(8,128)S(1)}, f32[2,128,8,4096]{3,1,2,0:T(8,128)}) fusion(pred[128,4096]{1,0:T(8,128)(4,1)S(1)} %copy-done.2, bf16[4096,2,128,1]{2,0,3,1:T(8,128)(2,1)S(1)} %bitcast.168, bf16[128,2,8,64]{3,0,2,1:T(8,128)(2,1)S(1)} %bitcast.171, bf16[128,2,8,64]{3,0,2,1:T(8,128)(2,1)S(1)} %bitcast.169), kind=kOutput, calls=%fused_computation.3 | convolution fusion | flops 2173696000 | bytes 36708352 | tf_op jit(solution)/shard_map/qkgd,skd->kgqs/dot_general | solution.py:48
  210.1 38.8 %all-gather.8.cloned.1.call-done = bf16[4096,2,128]{2,0,1:T(8,128)(2,1)} async-done(((bf16[128,2,128]{2,0,1:T(8,128)(2,1)}), bf16[4096,2,128]{2,0,1:T(8,128)(2,1)}) %all-gather.8.cloned.1.call-update) | async-done | bytes 2097168 | tf_op jit(solution)/shard_map/all_gather | solution.py:145
  249.0 15.0 %fusion.3 = (f32[2,8,128]{2,1,0:T(8,128)S(1)}, f32[2,4096,128,8]{2,1,3,0:T(8,128)}) fusion(pred[128,4096]{0,1:T(8,128)(4,1)} %fusion.29, bf16[128,2,8,64]{3,0,2,1:T(8,128)(2,1)} %bitcast.172, bf16[128,2,8,64]{3,0,2,1:T(8,128)(2,1)} %bitcast.170, bf16[4096,2,128]{2,0,1:T(8,128)(2,1)} %all-gather.8.cloned.1.call-done), kind=kOutput, calls=%fused_computation.10 | convolution fusion | flops 2173696000 | bytes 36708352 | tf_op jit(solution)/shard_map/qkgd,skd->kgqs/dot_general | solution.py:48
  264.0 16.4 %fusion.1 = f32[2,8,128]{2,1,0:T(8,128)S(1)} fusion(f32[2,4096,128,8]{2,1,3,0:T(8,128)} %get-tuple-element.22, f32[2,8,128]{2,1,0:T(8,128)S(1)} %get-tuple-element.16, pred[128,4096]{0,1:T(8,128)(4,1)S(1)} %copy-done.4), kind=kLoop, calls=%fused_computation.8 | loop fusion | flops 33552384 | bytes 34095104 | tf_op jit(solution)/shard_map/reduce_sum | solution.py:54
  280.3 3.9 copy-done.1
  284.2 9.5 %fusion.4 = f32[2,8,128]{2,1,0:T(8,128)S(1)} fusion(f32[2,128,8,4096]{3,1,2,0:T(8,128)S(1)} %copy-done.1, f32[2,8,128]{2,1,0:T(8,128)S(1)} %get-tuple-element.15, pred[128,4096]{1,0:T(8,128)(4,1)S(1)} %copy-done.3), kind=kLoop, calls=%fused_computation.11 | loop fusion | flops 33552384 | bytes 34095104 | tf_op jit(solution)/shard_map/reduce_sum | solution.py:54
  293.8 28.9 %all-gather.10.cloned.1.call-done = bf16[4096,2,128]{0,2,1:T(8,128)(2,1)} async-done(((bf16[128,2,128]{0,2,1:T(8,128)(2,1)}), bf16[4096,2,128]{0,2,1:T(8,128)(2,1)}) %all-gather.10.cloned.1.call-update) | async-done | bytes 2097168 | tf_op jit(solution)/shard_map/all_gather | solution.py:146
  322.7 16.3 %fusion.50 = f32[128,2,8,128]{0,3,2,1:T(8,128)} fusion(f32[2,4096,128,8]{2,1,3,0:T(8,128)} %get-tuple-element.22, f32[2,8,128]{2,1,0:T(8,128)S(1)} %get-tuple-element.16, pred[128,4096]{0,1:T(8,128)(4,1)} %fusion.29, bf16[4096,2,128]{0,2,1:T(8,128)(2,1)} %all-gather.10.cloned.1.call-done, f32[128,2,8]{0,2,1:T(8,128)S(1)} %get-tuple-element.5, ...), kind=kOutput, calls=%fused_computation.45 | convolution fusion | flops 2181562368 | bytes 37249024 | tf_op jit(solution)/shard_map/kgqs,skd->kgqd/dot_general | solution.py:55
  339.0 16.3 %fusion.60 = bf16[128,2,8,128]{0,3,2,1:T(8,128)(2,1)} fusion(f32[128,2,8,128]{0,3,2,1:T(8,128)} %fusion.50, bf16[4096,2,128,1]{0,2,1,3:T(8,128)(2,1)} %reshape.374, f32[2,128,8,4096]{3,1,2,0:T(8,128)} %get-tuple-element.20, f32[2,8,128]{2,1,0:T(8,128)S(1)} %get-tuple-element.15, pred[128,4096]{1,0:T(8,128)(4,1)} %broadcast_compare_fusion, ...), kind=kOutput, calls=%fused_computation.47 | convolution fusion | flops 2181824512 | bytes 37765120 | tf_op jit(solution)/shard_map/kgqs,skd->kgqd/dot_general | solution.py:55
  355.4 73.6 %all-gather.14.cloned.1.call-done = bf16[2048,2048]{1,0:T(8,128)(2,1)} async-done(((bf16[64,2048]{1,0:T(8,128)(2,1)}), bf16[2048,2048]{1,0:T(8,128)(2,1)}) %all-gather.14.cloned.1.call-update) | async-done | bytes 8388624 | tf_op jit(solution)/shard_map/all_gather | solution.py:177
  429.0 4.9 multiply_reduce_fusion
  433.9 1.0 copy-done.5
  434.9 0.9 multiply_convert_fusion
  435.9 10.9 %scatter_custom_fusion = bf16[1536,2048]{1,0:T(8,128)(2,1)} fusion(s32[1024]{0:T(1024)S(1)} %bitcast.176, bf16[]{:T(256)} %constant.80.clone.1, bf16[128,2048]{1,0:T(8,128)(2,1)} %multiply_convert_fusion), kind=kCustom, calls=%fused_computation.24 | custom fusion | bytes 6815746 | tf_op jit(solution)/shard_map/scatter | solution.py:190
  446.8 10.6 %reshape.350 = bf16[128,12,2048]{2,1,0:T(8,128)(2,1)} reshape(bf16[1536,2048]{1,0:T(8,128)(2,1)} %scatter_custom_fusion) | data formatting | bytes 12582912 | tf_op jit(solution)/shard_map/reshape | solution.py:194
  457.4 105.0 %all_to_all.10 = bf16[128,12,2048]{2,1,0:T(8,128)(2,1)} all-to-all(bf16[128,12,2048]{2,1,0:T(8,128)(2,1)} %reshape.350), channel_id=1, replica_groups=mesh['dp'=4,'expert'=32] {'dp','expert'}, dimensions={0} | all-to-all | bytes 12582912 | tf_op jit(solution)/shard_map/all_to_all | solution.py:193
  562.4 10.7 %reshape.351 = bf16[1536,2048]{1,0:T(8,128)(2,1)} reshape(bf16[128,12,2048]{2,1,0:T(8,128)(2,1)} %all_to_all.10) | data formatting | bytes 12582912 | tf_op jit(solution)/shard_map/reshape | solution.py:200
  573.1 14.1 %fusion.13 = f32[1536,1536]{1,0:T(8,128)S(1)} fusion(bf16[1536,2048]{1,0:T(8,128)(2,1)} %reshape.351, bf16[1,2048,1536]{2,1,0:T(8,128)(2,1)} %param.22), kind=kOutput, calls=%fused_computation.20 | convolution fusion | flops 9663676416 | bytes 22020096 | tf_op jit(solution)/shard_map/dot_general | solution.py:65
  587.3 7.1 convolution_convert_fusion
  594.3 10.6 %reshape.352 = bf16[128,12,2048]{2,1,0:T(8,128)(2,1)} reshape(bf16[1536,2048]{1,0:T(8,128)(2,1)} %convolution_convert_fusion) | data formatting | bytes 12582912 | tf_op jit(solution)/shard_map/reshape | solution.py:200
  604.9 7.6 %all-to-all-start.1 = ((bf16[128,12,2048]{2,1,0:T(8,128)(2,1)}), bf16[128,12,2048]{2,1,0:T(8,128)(2,1)}, u32[]{:S(2)}, u32[]{:S(2)}) async-start(bf16[128,12,2048]{2,1,0:T(8,128)(2,1)} %reshape.352), calls=%async_computation.1 | async-start | bytes 16777216 | tf_op jit(solution)/shard_map/all_to_all | solution.py:201
  613.5 104.1 %all-to-all-done.1 = bf16[128,12,2048]{2,1,0:T(8,128)(2,1)} async-done(((bf16[128,12,2048]{2,1,0:T(8,128)(2,1)}), bf16[128,12,2048]{2,1,0:T(8,128)(2,1)}, u32[]{:S(2)}, u32[]{:S(2)}) %all-to-all-start.1) | async-done | bytes 6291488 | tf_op jit(solution)/shard_map/all_to_all | solution.py:201
  717.5 10.7 %reshape.353 = bf16[1536,2048]{1,0:T(8,128)(2,1)} reshape(bf16[128,12,2048]{2,1,0:T(8,128)(2,1)} %all-to-all-done.1) | data formatting | bytes 12582912 | tf_op jit(solution)/shard_map/reshape | solution.py:202
  728.2 12.4 %gather_fusion = bf16[1024,2048]{1,0:T(8,128)(2,1)} fusion(bf16[1536,2048]{1,0:T(8,128)(2,1)} %reshape.353, s32[1024]{0:T(1024)S(1)} %broadcast_clamp_fusion), kind=kCustom, calls=%fused_computation | custom fusion | bytes 8392704 | tf_op jit(solution)/shard_map/gather | solution.py:202
  740.7 6.5 fusion.12
  747.2 2.2 add_convert_fusion
  (101 shorter events, 11.1 us)
Async XLA Ops:
  7.2 580.1 %copy-start = (bf16[1,768,2048]{2,1,0:T(8,128)(2,1)S(1)}, bf16[1,768,2048]{2,1,0:T(8,128)(2,1)}, u32[]{:S(2)}) copy-start(bf16[1,768,2048]{2,1,0:T(8,128)(2,1)} %param.23) | copy-start | bytes 9437188
  7.2 121.3 %all-gather.6.cloned.1.call-start = ((), (), s32[]{:S(2)}) async-start(), calls=%async_computation.2 | async-start | bytes 10813440 | tf_op jit(solution)/shard_map/all_gather | solution.py:105
  7.9 167.6 %all-gather.12.cloned.1.call-start = ((), (), s32[]{:S(2)}) async-start(), calls=%async_computation.5 | async-start | bytes 5242880 | tf_op jit(solution)/shard_map/all_gather | solution.py:153
  10.6 238.4 %all-gather.8.cloned.1.call-start = ((), (), s32[]{:S(2)}) async-start(), calls=%async_computation.3 | async-start | bytes 2162688 | tf_op jit(solution)/shard_map/all_gather | solution.py:145
  14.0 124.9 %copy-start.21 = (f32[128]{0:T(128)S(1)}, f32[128]{0:T(128)}, u32[]{:S(2)}) copy-start(f32[128]{0:T(128)} %param.19) | copy-start | bytes 1540
  14.0 129.0 %copy-start.18 = (s32[128,8]{0,1:T(8,128)S(1)}, s32[128,8]{0,1:T(8,128)}, u32[]{:S(2)}) copy-start(s32[128,8]{0,1:T(8,128)} %param.28) | copy-start | bytes 12292
  14.0 132.2 %copy-start.23 = (s32[32]{0:T(128)S(1)}, s32[32]{0:T(128)}, u32[]{:S(2)}) copy-start(s32[32]{0:T(128)} %param.25) | copy-start | bytes 388
  134.3 1.1 copy-start.8
  139.1 0.6 copy-start.12
  139.1 0.6 copy-start.14
  140.5 182.2 %all-gather.10.cloned.1.call-start = ((), (), s32[]{:S(2)}) async-start(), calls=%async_computation.4 | async-start | bytes 2162688 | tf_op jit(solution)/shard_map/all_gather | solution.py:146
  141.5 1.4 copy-start.16
  142.2 286.7 %all-gather.14.cloned.1.call-start = ((), (), s32[]{:S(2)}) async-start(), calls=%async_computation.6 | async-start | bytes 8650752 | tf_op jit(solution)/shard_map/all_gather | solution.py:177
  143.5 0.8 copy-start.11
  179.5 13.5 %copy-start.22 = (f32[128]{0:T(128)S(1)}, f32[128]{0:T(128)}, u32[]{:S(2)}) copy-start(f32[128]{0:T(128)} %param.18) | copy-start | bytes 1540
  191.5 1.0 copy-start.6
  193.0 3.4 copy-start.2
  193.1 3.4 copy-start.7
  195.5 0.8 copy-start.9
  195.6 0.9 copy-start.10
  249.0 15.0 %copy-start.4 = (pred[128,4096]{0,1:T(8,128)(4,1)S(1)}, pred[128,4096]{0,1:T(8,128)(4,1)}, u32[]{:S(2)}) copy-start(pred[128,4096]{0,1:T(8,128)(4,1)} %fusion.29) | copy-start | bytes 1572868
  263.9 20.3 %copy-start.1 = (f32[2,128,8,4096]{3,1,2,0:T(8,128)S(1)}, f32[2,128,8,4096]{3,1,2,0:T(8,128)}, u32[]{:S(2)}) copy-start(f32[2,128,8,4096]{3,1,2,0:T(8,128)} %get-tuple-element.20) | copy-start | bytes 100663296
  264.0 20.3 %copy-start.3 = (pred[128,4096]{1,0:T(8,128)(4,1)S(1)}, pred[128,4096]{1,0:T(8,128)(4,1)}, u32[]{:S(2)}) copy-start(pred[128,4096]{1,0:T(8,128)(4,1)} %broadcast_compare_fusion) | copy-start | bytes 1572868
  429.0 6.0 copy-start.19
  433.9 1.0 copy-start.5
  604.9 7.7 %copy-start.20 = (f32[128,8]{0,1:T(8,128)S(1)}, f32[128,8]{0,1:T(8,128)}, u32[]{:S(2)}) copy-start(f32[128,8]{0,1:T(8,128)} %param.29) | copy-start | bytes 12292
  604.9 7.8 %copy-start.13 = (bf16[128,2,64]{2,0,1:T(8,128)(2,1)S(1)}, bf16[128,2,64]{2,0,1:T(8,128)(2,1)}, u32[]{:S(2)}) copy-start(bf16[128,2,64]{2,0,1:T(8,128)(2,1)} %copy-done.12) | copy-start | bytes 98308
  604.9 7.8 %copy-start.15 = (bf16[128,2,64]{2,0,1:T(8,128)(2,1)S(1)}, bf16[128,2,64]{2,0,1:T(8,128)(2,1)}, u32[]{:S(2)}) copy-start(bf16[128,2,64]{2,0,1:T(8,128)(2,1)} %copy-done.14) | copy-start | bytes 98308
  604.9 7.9 %copy-start.17 = (bf16[128,256]{1,0:T(8,128)(2,1)S(1)}, bf16[128,256]{1,0:T(8,128)(2,1)}, u32[]{:S(2)}) copy-start(bf16[128,256]{1,0:T(8,128)(2,1)} %copy-done.16) | copy-start | bytes 196612
  604.9 112.6 %all-to-all-start.1 = ((bf16[128,12,2048]{2,1,0:T(8,128)(2,1)}), bf16[128,12,2048]{2,1,0:T(8,128)(2,1)}, u32[]{:S(2)}, u32[]{:S(2)}) async-start(bf16[128,12,2048]{2,1,0:T(8,128)(2,1)} %reshape.352), calls=%async_computation.1 | async-start | bytes 16777216 | tf_op jit(solution)/shard_map/all_to_all | solution.py:201
Sparse Core Ops, SparseCore 0:
  11.1 117.4 all-gather.5
  130.2 45.2 all-gather.11
  179.3 69.6 all-gather.7
  251.6 71.0 all-gather.9
  325.6 103.2 all-gather.13
where the time goes:
time: 762 us; the launch traced here: 756 us
  waiting for transfers between devices  382 us (50%)
  blocking collectives  105 us (14%)
  local copies, waits for them, and re-layouts  102 us (13%)
  matrix products  93.2 us (12%)
  other arithmetic  51.6 us (7%)
  between operations  14.5 us (2%)
  starting transfers between devices  7.85 us (1%)
    all_gather x1, waiting for transfers between devices, local(): lax.all_gather(query_key_value_weight, 'expert', axis=0, tiled=True)  114 us
    all_to_all x1, blocking collectives, local(): lax.all_to_all(outgoing.reshape(expert_count, capacity, width), ('dp', 'e...  105 us
    all_to_all x1, waiting for transfers between devices, local(): lax.all_to_all(results, ('dp', 'expert'), split_axis=0, concat_axis=0, ti...  104 us
    all_gather x1, waiting for transfers between devices, local(): lax.all_gather(w_out, 'expert', axis=0, tiled=True)  73.6 us
    all_gather x1, waiting for transfers between devices, local(): piece_keys = lax.all_gather(key_rows, 'expert', axis=0, tiled=True)  38.8 us
    dot_general x2, matrix products, attend(): jnp.einsum('kgqs,skd->kgqd', weights.astype(jnp.bfloat16), value_rows, pr...  32.7 us
    all_gather x1, waiting for transfers between devices, local(): piece_values = lax.all_gather(value_rows, 'expert', axis=0, tiled=True)  28.9 us
    dot_general x2, matrix products, attend(): jnp.einsum('qkgd,skd->kgqs', queries, key_rows, preferred_element_type=jn...  28.6 us
  transfers between devices with their start and end apart: 6, of which 6 were waited for; matrix products, arithmetic and copies ran while one was open for 18% of the time, Pallas kernels for 0%

commit v1 on v0

--- a/solution.py
+++ b/solution.py
@@ -142,8 +142,13 @@
         jnp.zeros((kv_heads, head_split, tokens_here), jnp.float32),
         jnp.zeros((kv_heads, head_split, tokens_here, head_dim), jnp.float32),
     )
-    piece_keys = lax.all_gather(key_rows, "expert", axis=0, tiled=True)
-    piece_values = lax.all_gather(value_rows, "expert", axis=0, tiled=True)
+    piece_keys, piece_values = jnp.split(
+        lax.all_gather(
+            jnp.concatenate([key_rows, value_rows], axis=1), "expert", axis=0, tiled=True
+        ),
+        [key_rows.shape[1]],
+        axis=1,
+    )
     key_index = jnp.arange(piece_keys.shape[0], dtype=jnp.int32)
     key_request, _, _ = layout(lengths_row, key_index)
     mask = (key_request[None, :] == request[:, None]) & (key_index[None, :] <= index[:, None])

time: 762 us -> 698 us (0.916)
  waiting for transfers between devices: 382 us -> 318 us
    all_gather x1, waiting for transfers between devices: 73.6 us -> 27.9 us  [local(): lax.all_gather(w_out, 'expert', axis=0, tiled=True)]
    all_gather x2 -> x1, waiting for transfers between devices: 67.8 us -> 49.5 us  [local(): lax.all_gather(jnp.concatenate([key_rows, value_rows], axis=1), 'expert',...]
  transfers between devices with their start and end apart: 6 -> 5, of which waited for: 6 -> 5; matrix products, arithmetic and copies ran while one was open for 18% -> 20% of each run, Pallas kernels for 0% -> 0%
where the time goes in v1:
time: 698 us; the launch traced here: 693 us
  waiting for transfers between devices  318 us (46%)
  blocking collectives  105 us (15%)
  local copies, waits for them, and re-layouts  102 us (15%)
  matrix products  93.6 us (13%)
  other arithmetic  51.6 us (7%)
  between operations  14.5 us (2%)
  starting transfers between devices  7.79 us (1%)
    all_gather x1, waiting for transfers between devices, local(): lax.all_gather(query_key_value_weight, 'expert', axis=0, tiled=True)  114 us
    all_to_all x1, blocking collectives, local(): lax.all_to_all(outgoing.reshape(expert_count, capacity, width), ('dp', 'e...  105 us
    all_to_all x1, waiting for transfers between devices, local(): lax.all_to_all(results, ('dp', 'expert'), split_axis=0, concat_axis=0, ti...  103 us
    all_gather x1, waiting for transfers between devices, local(): lax.all_gather(jnp.concatenate([key_rows, value_rows], axis=1), 'expert',...  49.5 us
    dot_general x2, matrix products, attend(): jnp.einsum('kgqs,skd->kgqd', weights.astype(jnp.bfloat16), value_rows, pr...  33 us
    dot_general x2, matrix products, attend(): jnp.einsum('qkgd,skd->kgqs', queries, key_rows, preferred_element_type=jn...  28.8 us
    all_gather x1, waiting for transfers between devices, local(): lax.all_gather(w_out, 'expert', axis=0, tiled=True)  27.9 us
    reduce_sum x2, other arithmetic, attend(): total = total * scale_factor + jnp.sum(weights, axis=-1)  25.9 us
  transfers between devices with their start and end apart: 5, of which 5 were waited for; matrix products, arithmetic and copies ran while one was open for 20% of the time, Pallas kernels for 0%

profile of v1, /device:TPU:67, one launch (start us, length us, event | category | flops | bytes accessed | tf_op | source)
XLA Modules:
  0.0 692.7 jit_solution(10252315292533270627)
XLA Ops:
  8.0 2.7 copy.103
  12.5 1.2 fusion.57
  14.1 114.4 %all-gather.5.cloned.1.call-done = bf16[2048,2560]{1,0:T(8,128)(2,1)} async-done(((bf16[64,2560]{1,0:T(8,128)(2,1)}), bf16[2048,2560]{1,0:T(8,128)(2,1)}) %all-gather.5.cloned.1.call-update) | async-done | bytes 10485776 | tf_op jit(solution)/shard_map/all_gather | solution.py:105
  128.5 5.7 fusion.60
  134.3 1.1 copy-done.7
  136.0 1.6 reshape.345
  137.6 1.1 multiply_reduce_fusion.2
  139.8 0.9 copy_bitcast_fusion.1
  142.7 0.8 copy-done.8
  143.5 1.9 broadcast_add_fusion
  145.6 1.9 copy.110
  147.7 1.4 fusion.63
  149.2 1.2 broadcast_compare_fusion
  150.4 3.1 fusion.27
  153.5 22.0 %all-gather.9.cloned.1.call-done = bf16[32,2,128,2,128]{4,2,3,1,0:T(8,128)(2,1)} async-done(((bf16[8,2,128,2,128]{4,2,3,1,0:T(8,128)(2,1)}), bf16[32,2,128,2,128]{4,2,3,1,0:T(8,128)(2,1)}) %all-gather.9.cloned.1.call-update) | async-done | bytes 4194320 | tf_op jit(solution)/shard_map/all_gather | solution.py:158
  175.5 4.1 fusion.86
  179.5 1.6 copy.104
  181.2 4.6 copy.105
  185.8 4.2 reshape.374
  190.0 1.3 slice_bitcast_fusion.10
  191.5 1.0 copy-done.5
  193.1 1.7 multiply_multiply_fusion
  196.5 13.7 %bitcast_reduce_fusion = (f32[2,8,128]{2,1,0:T(8,128)S(1)}, f32[2,128,8,4096]{3,1,2,0:T(8,128)}) fusion(pred[128,4096]{1,0:T(8,128)(4,1)S(1)} %copy-done.2, bf16[4096,2,128,1]{2,0,3,1:T(8,128)(2,1)S(1)} %bitcast.172, bf16[128,2,8,64]{3,0,2,1:T(8,128)(2,1)S(1)} %bitcast.175, bf16[128,2,8,64]{3,0,2,1:T(8,128)(2,1)S(1)} %bitcast.173), kind=kOutput, calls=%fused_computation.3 | convolution fusion | flops 2173696000 | bytes 36708352 | tf_op jit(solution)/shard_map/qkgd,skd->kgqs/dot_general | solution.py:48
  210.1 49.5 %all-gather.7.cloned.1.call-done = bf16[4096,4,128]{2,0,1:T(8,128)(2,1)} async-done(((bf16[128,4,128]{2,0,1:T(8,128)(2,1)}), bf16[4096,4,128]{2,0,1:T(8,128)(2,1)}) %all-gather.7.cloned.1.call-update) | async-done | bytes 4194320 | tf_op jit(solution)/shard_map/all_gather | solution.py:146
  259.7 15.1 %fusion.3 = (f32[2,8,128]{2,1,0:T(8,128)S(1)}, f32[2,4096,128,8]{2,1,3,0:T(8,128)}) fusion(pred[128,4096]{0,1:T(8,128)(4,1)} %fusion.27, bf16[128,2,8,64]{3,0,2,1:T(8,128)(2,1)} %bitcast.176, bf16[128,2,8,64]{3,0,2,1:T(8,128)(2,1)} %bitcast.174, bf16[4096,4,128]{2,0,1:T(8,128)(2,1)} %all-gather.7.cloned.1.call-done), kind=kOutput, calls=%fused_computation.10 | convolution fusion | flops 2173696000 | bytes 37232640 | tf_op jit(solution)/shard_map/qkgd,skd->kgqs/dot_general | solution.py:48
  274.8 16.4 %fusion.1 = f32[2,8,128]{2,1,0:T(8,128)S(1)} fusion(f32[2,4096,128,8]{2,1,3,0:T(8,128)} %get-tuple-element.22, f32[2,8,128]{2,1,0:T(8,128)S(1)} %get-tuple-element.16, pred[128,4096]{0,1:T(8,128)(4,1)S(1)} %copy-done.9), kind=kLoop, calls=%fused_computation.8 | loop fusion | flops 33552384 | bytes 34095104 | tf_op jit(solution)/shard_map/reduce_sum | solution.py:54
  291.2 3.9 copy-done.1
  295.1 9.5 %fusion.4 = f32[2,8,128]{2,1,0:T(8,128)S(1)} fusion(f32[2,128,8,4096]{3,1,2,0:T(8,128)S(1)} %copy-done.1, f32[2,8,128]{2,1,0:T(8,128)S(1)} %get-tuple-element.15, pred[128,4096]{1,0:T(8,128)(4,1)S(1)} %copy-done.3), kind=kLoop, calls=%fused_computation.11 | loop fusion | flops 33552384 | bytes 34095104 | tf_op jit(solution)/shard_map/reduce_sum | solution.py:54
  304.7 16.4 %fusion.44 = f32[128,2,8,128]{0,3,2,1:T(8,128)} fusion(bf16[4096,4,128]{2,0,1:T(8,128)(2,1)} %all-gather.7.cloned.1.call-done, f32[2,4096,128,8]{2,1,3,0:T(8,128)} %get-tuple-element.22, f32[2,8,128]{2,1,0:T(8,128)S(1)} %get-tuple-element.16, pred[128,4096]{0,1:T(8,128)(4,1)} %fusion.27, f32[128,2,8]{0,2,1:T(8,128)S(1)} %get-tuple-element.5, ...), kind=kOutput, calls=%fused_computation.45 | convolution fusion | flops 2181562368 | bytes 37249024 | tf_op jit(solution)/shard_map/kgqs,skd->kgqd/dot_general | solution.py:55
  321.1 16.6 %fusion.52 = bf16[128,2,8,128]{0,3,2,1:T(8,128)(2,1)} fusion(f32[128,2,8,128]{0,3,2,1:T(8,128)} %fusion.44, bf16[4096,2,128,1]{0,2,1,3:T(8,128)(2,1)} %reshape.374, f32[2,128,8,4096]{3,1,2,0:T(8,128)} %get-tuple-element.20, f32[2,8,128]{2,1,0:T(8,128)S(1)} %get-tuple-element.15, pred[128,4096]{1,0:T(8,128)(4,1)} %broadcast_compare_fusion, ...), kind=kOutput, calls=%fused_computation.47 | convolution fusion | flops 2181824512 | bytes 37765120 | tf_op jit(solution)/shard_map/kgqs,skd->kgqd/dot_general | solution.py:55
  337.6 27.9 %all-gather.11.cloned.1.call-done = bf16[2048,2048]{1,0:T(8,128)(2,1)} async-done(((bf16[64,2048]{1,0:T(8,128)(2,1)}), bf16[2048,2048]{1,0:T(8,128)(2,1)}) %all-gather.11.cloned.1.call-update) | async-done | bytes 8388624 | tf_op jit(solution)/shard_map/all_gather | solution.py:182
  365.5 4.9 multiply_reduce_fusion
  370.5 1.0 copy-done.4
  371.5 0.9 multiply_convert_fusion
  372.4 10.9 %scatter_custom_fusion = bf16[1536,2048]{1,0:T(8,128)(2,1)} fusion(s32[1024]{0:T(1024)S(1)} %bitcast.179, bf16[]{:T(256)} %constant.80.clone.1, bf16[128,2048]{1,0:T(8,128)(2,1)} %multiply_convert_fusion), kind=kCustom, calls=%fused_computation.24 | custom fusion | bytes 6815746 | tf_op jit(solution)/shard_map/scatter | solution.py:195
  383.3 10.6 %reshape.350 = bf16[128,12,2048]{2,1,0:T(8,128)(2,1)} reshape(bf16[1536,2048]{1,0:T(8,128)(2,1)} %scatter_custom_fusion) | data formatting | bytes 12582912 | tf_op jit(solution)/shard_map/reshape | solution.py:199
  393.9 105.0 %all_to_all.10 = bf16[128,12,2048]{2,1,0:T(8,128)(2,1)} all-to-all(bf16[128,12,2048]{2,1,0:T(8,128)(2,1)} %reshape.350), channel_id=1, replica_groups=mesh['dp'=4,'expert'=32] {'dp','expert'}, dimensions={0} | all-to-all | bytes 12582912 | tf_op jit(solution)/shard_map/all_to_all | solution.py:198
  498.9 10.7 %reshape.351 = bf16[1536,2048]{1,0:T(8,128)(2,1)} reshape(bf16[128,12,2048]{2,1,0:T(8,128)(2,1)} %all_to_all.10) | data formatting | bytes 12582912 | tf_op jit(solution)/shard_map/reshape | solution.py:205
  509.6 14.1 %fusion.13 = f32[1536,1536]{1,0:T(8,128)S(1)} fusion(bf16[1536,2048]{1,0:T(8,128)(2,1)} %reshape.351, bf16[1,2048,1536]{2,1,0:T(8,128)(2,1)} %param.22), kind=kOutput, calls=%fused_computation.20 | convolution fusion | flops 9663676416 | bytes 22020096 | tf_op jit(solution)/shard_map/dot_general | solution.py:65
  523.8 7.1 %convolution_convert_fusion = bf16[1536,2048]{1,0:T(8,128)(2,1)} fusion(bf16[1,768,2048]{2,1,0:T(8,128)(2,1)S(1)} %copy-done, f32[1536,1536]{1,0:T(8,128)S(1)} %fusion.13), kind=kOutput, calls=%fused_computation.19 | convolution fusion | flops 4842061824 | bytes 18874368 | tf_op jit(solution)/shard_map/dot_general | solution.py:68
  530.9 10.6 %reshape.352 = bf16[128,12,2048]{2,1,0:T(8,128)(2,1)} reshape(bf16[1536,2048]{1,0:T(8,128)(2,1)} %convolution_convert_fusion) | data formatting | bytes 12582912 | tf_op jit(solution)/shard_map/reshape | solution.py:205
  541.4 7.6 %all-to-all-start.1 = ((bf16[128,12,2048]{2,1,0:T(8,128)(2,1)}), bf16[128,12,2048]{2,1,0:T(8,128)(2,1)}, u32[]{:S(2)}, u32[]{:S(2)}) async-start(bf16[128,12,2048]{2,1,0:T(8,128)(2,1)} %reshape.352), calls=%async_computation.1 | async-start | bytes 16777216 | tf_op jit(solution)/shard_map/all_to_all | solution.py:206
  549.2 0.9 slice.85
  550.9 103.2 %all-to-all-done.1 = bf16[128,12,2048]{2,1,0:T(8,128)(2,1)} async-done(((bf16[128,12,2048]{2,1,0:T(8,128)(2,1)}), bf16[128,12,2048]{2,1,0:T(8,128)(2,1)}, u32[]{:S(2)}, u32[]{:S(2)}) %all-to-all-start.1) | async-done | bytes 6291488 | tf_op jit(solution)/shard_map/all_to_all | solution.py:206
  654.1 10.7 %reshape.353 = bf16[1536,2048]{1,0:T(8,128)(2,1)} reshape(bf16[128,12,2048]{2,1,0:T(8,128)(2,1)} %all-to-all-done.1) | data formatting | bytes 12582912 | tf_op jit(solution)/shard_map/reshape | solution.py:207
  664.8 12.4 %gather_fusion = bf16[1024,2048]{1,0:T(8,128)(2,1)} fusion(bf16[1536,2048]{1,0:T(8,128)(2,1)} %reshape.353, s32[1024]{0:T(1024)S(1)} %broadcast_clamp_fusion), kind=kCustom, calls=%fused_computation | custom fusion | bytes 8392704 | tf_op jit(solution)/shard_map/gather | solution.py:207
  677.2 6.5 fusion.12
  683.7 2.2 add_convert_fusion
  (95 shorter events, 10.3 us)
Async XLA Ops:
  7.2 516.6 %copy-start = (bf16[1,768,2048]{2,1,0:T(8,128)(2,1)S(1)}, bf16[1,768,2048]{2,1,0:T(8,128)(2,1)}, u32[]{:S(2)}) copy-start(bf16[1,768,2048]{2,1,0:T(8,128)(2,1)} %param.23) | copy-start | bytes 9437188
  7.2 121.3 %all-gather.5.cloned.1.call-start = ((), (), s32[]{:S(2)}) async-start(), calls=%async_computation.2 | async-start | bytes 10813440 | tf_op jit(solution)/shard_map/all_gather | solution.py:105
  7.9 167.6 %all-gather.9.cloned.1.call-start = ((), (), s32[]{:S(2)}) async-start(), calls=%async_computation.4 | async-start | bytes 5242880 | tf_op jit(solution)/shard_map/all_gather | solution.py:158
  10.7 249.0 %all-gather.7.cloned.1.call-start = ((), (), s32[]{:S(2)}) async-start(), calls=%async_computation.3 | async-start | bytes 4325376 | tf_op jit(solution)/shard_map/all_gather | solution.py:146
  14.1 124.8 %copy-start.19 = (f32[128]{0:T(128)S(1)}, f32[128]{0:T(128)}, u32[]{:S(2)}) copy-start(f32[128]{0:T(128)} %param.19) | copy-start | bytes 1540
  14.1 128.1 %copy-start.16 = (s32[128,8]{0,1:T(8,128)S(1)}, s32[128,8]{0,1:T(8,128)}, u32[]{:S(2)}) copy-start(s32[128,8]{0,1:T(8,128)} %param.28) | copy-start | bytes 12292
  14.1 131.3 %copy-start.21 = (s32[32]{0:T(128)S(1)}, s32[32]{0:T(128)}, u32[]{:S(2)}) copy-start(s32[32]{0:T(128)} %param.25) | copy-start | bytes 388
  134.3 1.1 copy-start.7
  139.1 0.6 copy-start.12
  139.1 0.7 copy-start.14
  141.5 224.0 %all-gather.11.cloned.1.call-start = ((), (), s32[]{:S(2)}) async-start(), calls=%async_computation.5 | async-start | bytes 8650752 | tf_op jit(solution)/shard_map/all_gather | solution.py:182
  142.7 0.8 copy-start.8
  181.2 11.9 %copy-start.20 = (f32[128]{0:T(128)S(1)}, f32[128]{0:T(128)}, u32[]{:S(2)}) copy-start(f32[128]{0:T(128)} %param.18) | copy-start | bytes 1540
  191.5 1.0 copy-start.5
  193.1 3.4 copy-start.2
  193.1 3.4 copy-start.6
  195.5 0.8 copy-start.10
  195.6 0.8 copy-start.11
  259.7 15.1 %copy-start.9 = (pred[128,4096]{0,1:T(8,128)(4,1)S(1)}, pred[128,4096]{0,1:T(8,128)(4,1)}, u32[]{:S(2)}) copy-start(pred[128,4096]{0,1:T(8,128)(4,1)} %fusion.27) | copy-start | bytes 1572868
  274.8 20.3 %copy-start.1 = (f32[2,128,8,4096]{3,1,2,0:T(8,128)S(1)}, f32[2,128,8,4096]{3,1,2,0:T(8,128)}, u32[]{:S(2)}) copy-start(f32[2,128,8,4096]{3,1,2,0:T(8,128)} %get-tuple-element.20) | copy-start | bytes 100663296
  274.8 20.3 %copy-start.3 = (pred[128,4096]{1,0:T(8,128)(4,1)S(1)}, pred[128,4096]{1,0:T(8,128)(4,1)}, u32[]{:S(2)}) copy-start(pred[128,4096]{1,0:T(8,128)(4,1)} %broadcast_compare_fusion) | copy-start | bytes 1572868
  365.5 6.0 copy-start.17
  370.5 1.0 copy-start.4
  541.4 7.6 %copy-start.18 = (f32[128,8]{0,1:T(8,128)S(1)}, f32[128,8]{0,1:T(8,128)}, u32[]{:S(2)}) copy-start(f32[128,8]{0,1:T(8,128)} %param.29) | copy-start | bytes 12292
  541.4 8.7 %copy-start.13 = (bf16[128,2,64]{2,0,1:T(8,128)(2,1)S(1)}, bf16[128,2,64]{2,0,1:T(8,128)(2,1)}, u32[]{:S(2)}) copy-start(bf16[128,2,64]{2,0,1:T(8,128)(2,1)} %copy-done.12) | copy-start | bytes 98308
  541.4 8.7 %copy-start.15 = (bf16[128,2,64]{2,0,1:T(8,128)(2,1)S(1)}, bf16[128,2,64]{2,0,1:T(8,128)(2,1)}, u32[]{:S(2)}) copy-start(bf16[128,2,64]{2,0,1:T(8,128)(2,1)} %copy-done.14) | copy-start | bytes 98308
  541.4 112.6 %all-to-all-start.1 = ((bf16[128,12,2048]{2,1,0:T(8,128)(2,1)}), bf16[128,12,2048]{2,1,0:T(8,128)(2,1)}, u32[]{:S(2)}, u32[]{:S(2)}) async-start(bf16[128,12,2048]{2,1,0:T(8,128)(2,1)} %reshape.352), calls=%async_computation.1 | async-start | bytes 16777216 | tf_op jit(solution)/shard_map/all_to_all | solution.py:206
Sparse Core Ops, SparseCore 0:
  11.1 117.4 all-gather.4
  130.2 45.2 all-gather.8
  179.3 80.3 all-gather.6
  262.6 102.8 all-gather.10
